TPU v7x, 32 devices: a whole 2x2x4 slice. The times are simulated.
32 devices in a mesh: kx: 2 (over x), ky: 8 (over z, y), af: 2 (over core).
Axes of the slice: x: 2, y: 2, z: 4, core: 2. Of those that a mesh axis runs over, the one named last changes fastest.
Arguments:
- vertex: float32 [2, 2, 8, 768, 768], P(None, 'kx', 'ky', 'af'), may hold values from -1.2 to 1.2
- bare_vertex: float32 [2, 2, 8, 768, 768], P(None, 'kx', 'ky', 'af'), may hold values from -1.2 to 1.2
- bubble_direct: float32 [2, 2, 8, 768], P(None, 'kx', 'ky'), may hold values from 0.1 to 1
- bubble_crossed: float32 [2, 2, 8, 768], P(None, 'kx', 'ky'), may hold values from 0.1 to 1
- shear_in: int32 [2, 768], replicated, may hold values from 0 to 7, as said below
- shear_out: int32 [2, 768], replicated, may hold values from 0 to 7, as said below
Outputs:
- updated: float32 [2, 2, 8, 768, 768], P(None, 'kx', 'ky', 'af')
Inputs may be any that keep to these rules, and one draw needn't show every extreme that they name: `shear_in`: row 0 holds each matrix row's shift of the first momentum component (below 4), row 1 that of the second (below 8). Within each half of the 768 rows, every pair (first shift mod 2, second shift) occurs for exactly 24 rows. `shear_out`: same structure as shear_in.
All inputs are finite; a program needn't handle non-finite values.
Results may differ from a plain program's by a relative error of at most 0.000082.
Values sent between devices are 32-bit elements; how exact they have to be, the bound alone decides.
No kernel may reach another device: no remote copies, remote signals or barrier semaphores. Data moves between devices by JAX's collectives and lax.ppermute only.
A program may use at most 64 MiB of HBM per device.

v0:
```python
import jax
import jax.numpy as jnp
from jax import lax
from jax.sharding import PartitionSpec as P

mixing = 0.5


def ladder(vertex_rows, bubble_row):
    scaled = vertex_rows * bubble_row[:, None, :]
    whole = lax.all_gather(vertex_rows, "af", axis=1, tiled=True)
    return jnp.einsum(
        "hrk,hkc->hrc",
        scaled,
        whole,
        precision=lax.Precision.HIGHEST,
        preferred_element_type=jnp.float32,
    )


def pack_rows(data, target):
    row_order = jnp.argsort(target, stable=True)
    return jnp.take(data, row_order, axis=1)


def unpack_rows(data, anchor):
    row_order = jnp.argsort(anchor, stable=True)
    inverse = jnp.argsort(row_order, stable=True)
    return jnp.take(data, inverse, axis=1)


def crossing(vertex_rows, shear_table):
    item_count = vertex_rows.shape[0]
    row_count = vertex_rows.shape[1]
    row_first = lax.axis_index("af") * row_count
    shift_x = lax.dynamic_slice_in_dim(shear_table[0], row_first, row_count)
    shift_y = lax.dynamic_slice_in_dim(shear_table[1], row_first, row_count)
    width_x = lax.axis_size("kx")
    width_y = lax.axis_size("ky")
    kx_index = lax.axis_index("kx")
    ky_index = lax.axis_index("ky")
    carry_bit = (kx_index + shift_x % width_x >= width_x).astype(jnp.int32)
    item_turn = (shift_x // width_x + carry_bit) % item_count
    turned = vertex_rows
    rolled = jnp.roll(vertex_rows, 1, axis=0)
    turned = jnp.where((item_turn == 1)[None, :, None], rolled, turned)
    target_x = (kx_index + shift_x) % width_x
    target_y = (ky_index + shift_y) % width_y
    anchor_x = (kx_index - shift_x) % width_x
    anchor_y = (ky_index - shift_y) % width_y
    arrived = lax.all_to_all(
        pack_rows(turned, target_x * width_y + target_y),
        ("kx", "ky"),
        split_axis=1,
        concat_axis=1,
        tiled=True,
    )
    return unpack_rows(arrived, anchor_x * width_y + anchor_y)


def body(vertex, bare_vertex, bubble_direct, bubble_crossed, shear_in, shear_out):
    item_count = vertex.shape[0]
    row_count = vertex.shape[3]
    columns = vertex.shape[4]
    local_field = vertex.reshape(item_count, row_count, columns)
    local_bare = bare_vertex.reshape(item_count, row_count, columns)
    direct_bubble = bubble_direct.reshape(item_count, columns)
    crossed_bubble = bubble_crossed.reshape(item_count, columns)
    direct_ladder = ladder(local_field, direct_bubble)
    crossed = crossing(local_field, shear_in)
    crossed_ladder = ladder(crossed, crossed_bubble)
    returned = crossing(crossed_ladder, shear_out)
    updated = (1.0 - mixing) * local_field + mixing * (local_bare + direct_ladder + returned)
    return updated.reshape(vertex.shape)


def solution(mesh):
    placed = (
        P(None, "kx", "ky", "af", None),
        P(None, "kx", "ky", "af", None),
        P(None, "kx", "ky", None),
        P(None, "kx", "ky", None),
        P(),
        P(),
    )
    return jax.shard_map(
        body, mesh=mesh, in_specs=placed, out_specs=P(None, "kx", "ky", "af", None), check_vma=False
    )
```

profile of v0, /device:TPU:0, one launch (start us, length us, event | category | flops | bytes accessed | tf_op | source)
XLA Modules:
  0.0 213.0 jit_solution(2897367871155619934)
XLA Ops:
  6.5 0.8 fusion.44
  7.4 3.8 %sort.87 = (s32[384]{0:T(512)}, s32[384]{0:T(512)S(1)}) sort(s32[384]{0:T(512)S(1)} %get-tuple-element.33, s32[384]{0:T(512)S(1)} %iota.19), dimensions={0}, to_apply=%region_0.1 | sort | flops 3456 | bytes 6144 | tf_op jit(solution)/shard_map/jit(argsort)/sort | solution.py:22
  11.2 0.0 copy-start
  11.2 1.9 slice_bitcast_fusion.1
  13.1 0.4 copy-done
  13.6 0.5 maximum_select_fusion
  14.1 3.2 %copy.10 = f32[2,384,768]{2,0,1:T(2,128)} copy(f32[2,384,768]{2,1,0:T(8,128)S(1)} %maximum_select_fusion) | data formatting | bytes 4718592 | tf_op jit(solution)/shard_map/jit(_where)/select_n | solution.py:46
  17.3 5.1 %gather_fusion = f32[384,2,768]{2,1,0:T(2,128)S(1)} fusion(f32[2,384,768]{2,0,1:T(2,128)} %copy.10, s32[1024]{0:T(1024)S(1)} %pad_clamp_fusion.3), kind=kCustom, calls=%fused_computation.clone | custom fusion | bytes 4720128 | tf_op jit(solution)/shard_map/jit(_take)/gather | solution.py:23
  22.4 2.8 %select_bitcast_fusion.1 = f32[2,384,768]{2,0,1:T(2,128)} fusion(f32[384,2,768]{2,1,0:T(2,128)S(1)} %gather_fusion, pred[384]{0:T(512)(128)(4,1)S(1)} %compare_and_fusion.3), kind=kLoop, calls=%fused_computation.18 | loop fusion | flops 589824 | bytes 4718976 | tf_op jit(solution)/shard_map/jit(_take)/select_n | solution.py:23
  25.1 8.3 %all-to-all-start = ((f32[2,384,768]{2,0,1:T(2,128)}), f32[2,384,768]{2,0,1:T(2,128)S(1)}, u32[]{:S(2)}, u32[]{:S(2)}) async-start(f32[2,384,768]{2,0,1:T(2,128)} %select_bitcast_fusion.1), calls=%async_computation | async-start | bytes 4718592 | tf_op jit(solution)/shard_map/all_to_all | solution.py:51
  33.5 0.0 all-gather.4.cloned.1.call-start
  33.5 3.8 %sort.88 = (s32[384]{0:T(512)}, s32[384]{0:T(512)S(1)}) sort(s32[384]{0:T(512)S(1)} %get-tuple-element.32, s32[384]{0:T(512)S(1)} %iota.20), dimensions={0}, to_apply=%region_1.3 | sort | flops 3456 | bytes 6144 | tf_op jit(solution)/shard_map/jit(argsort)/sort | solution.py:27
  37.3 3.8 %sort.89 = (s32[384]{0:T(512)}, s32[384]{0:T(512)S(1)}) sort(s32[384]{0:T(512)S(1)} %get-tuple-element.13, s32[384]{0:T(512)S(1)} %iota.21), dimensions={0}, to_apply=%region_2.4 | sort | flops 3456 | bytes 6144 | tf_op jit(solution)/shard_map/jit(argsort)/sort | solution.py:28
  41.1 44.8 %all-to-all-done = f32[2,384,768]{2,0,1:T(2,128)S(1)} async-done(((f32[2,384,768]{2,0,1:T(2,128)}), f32[2,384,768]{2,0,1:T(2,128)S(1)}, u32[]{:S(2)}, u32[]{:S(2)}) %all-to-all-start) | async-done | bytes 2359328 | tf_op jit(solution)/shard_map/all_to_all | solution.py:51
  85.9 5.2 %gather_fusion.1 = f32[384,2,768]{2,1,0:T(2,128)} fusion(f32[2,384,768]{2,0,1:T(2,128)S(1)} %all-to-all-done, s32[1024]{0:T(1024)S(1)} %pad_clamp_fusion.2), kind=kCustom, calls=%fused_computation.1.clone | custom fusion | bytes 4720128 | tf_op jit(solution)/shard_map/jit(_take)/gather | solution.py:29
  91.1 3.3 %fusion.5 = f32[2,384,768]{2,1,0:T(8,128)} fusion(f32[384,2,768]{2,1,0:T(2,128)} %gather_fusion.1, pred[384]{0:T(512)(128)(4,1)S(1)} %compare_and_fusion.2), kind=kLoop, calls=%fused_computation.16 | loop fusion | flops 589824 | bytes 4718976 | tf_op jit(solution)/shard_map/jit(_take)/select_n | solution.py:29
  94.4 0.0 copy-start.3
  94.4 0.0 copy-start.4
  94.4 0.0 copy-start.2
  94.4 0.0 all-gather.4.cloned.1.call-update
  94.5 0.2 all-gather.6.cloned.1.call-start
  94.7 0.5 all-gather.6.cloned.1.call-update
  95.2 0.0 copy-done.3
  95.4 3.8 %sort.90 = (s32[384]{0:T(512)}, s32[384]{0:T(512)S(1)}) sort(s32[384]{0:T(512)S(1)} %get-tuple-element.31, s32[384]{0:T(512)S(1)} %iota.22), dimensions={0}, to_apply=%region_3.5 | sort | flops 3456 | bytes 6144 | tf_op jit(solution)/shard_map/jit(argsort)/sort | solution.py:22
  99.1 0.0 copy-done.4
  99.2 9.8 %all-gather.4.cloned.1.call-done = f32[2,768,768]{2,1,0:T(8,128)} async-done(((f32[2,384,768]{2,1,0:T(8,128)}), f32[2,768,768]{2,1,0:T(8,128)}) %all-gather.4.cloned.1.call-update) | async-done | bytes 4718608 | tf_op jit(solution)/shard_map/all_gather | solution.py:11
  109.0 0.0 copy-done.2
  109.0 7.9 %fusion.6 = f32[2,384,768]{2,1,0:T(8,128)S(1)} fusion(f32[2,768,768]{2,1,0:T(8,128)} %all-gather.4.cloned.1.call-done, f32[2,384,768]{2,1,0:T(8,128)S(1)} %copy-done.2, f32[2,768]{1,0:T(2,128)S(1)} %bitcast.48), kind=kOutput, calls=%fused_computation.19 | convolution fusion | flops 5436407808 | bytes 9443328 | tf_op jit(solution)/shard_map/hrk,hkc->hrc/dot_general | solution.py:12
  116.9 0.2 fusion.42
  117.1 0.5 maximum_select_fusion.1
  117.6 3.2 %copy.12 = f32[2,384,768]{2,0,1:T(2,128)} copy(f32[2,384,768]{2,1,0:T(8,128)S(1)} %maximum_select_fusion.1) | data formatting | bytes 4718592 | tf_op jit(solution)/shard_map/jit(_where)/select_n | solution.py:46
  120.8 5.4 %gather_fusion.2 = f32[384,2,768]{2,1,0:T(2,128)S(1)} fusion(f32[2,384,768]{2,0,1:T(2,128)} %copy.12, s32[1024]{0:T(1024)S(1)} %pad_clamp_fusion.1), kind=kCustom, calls=%fused_computation.2.clone | custom fusion | bytes 4720128 | tf_op jit(solution)/shard_map/jit(_take)/gather | solution.py:23
  126.2 2.8 %select_bitcast_fusion = f32[2,384,768]{2,0,1:T(2,128)} fusion(f32[384,2,768]{2,1,0:T(2,128)S(1)} %gather_fusion.2, pred[384]{0:T(512)(128)(4,1)S(1)} %compare_and_fusion.1), kind=kLoop, calls=%fused_computation.17 | loop fusion | flops 589824 | bytes 4718976 | tf_op jit(solution)/shard_map/jit(_take)/select_n | solution.py:23
  128.9 0.0 copy-start.5
  128.9 7.0 %all-to-all-start.1 = ((f32[2,384,768]{2,0,1:T(2,128)}), f32[2,384,768]{2,0,1:T(2,128)}, u32[]{:S(2)}, u32[]{:S(2)}) async-start(f32[2,384,768]{2,0,1:T(2,128)} %select_bitcast_fusion), calls=%async_computation.1 | async-start | bytes 4718592 | tf_op jit(solution)/shard_map/all_to_all | solution.py:51
  135.9 0.0 copy-done.5
  136.0 3.8 %sort.91 = (s32[384]{0:T(512)}, s32[384]{0:T(512)S(1)}) sort(s32[384]{0:T(512)S(1)} %get-tuple-element.30, s32[384]{0:T(512)S(1)} %iota.23), dimensions={0}, to_apply=%region_4.6 | sort | flops 3456 | bytes 6144 | tf_op jit(solution)/shard_map/jit(argsort)/sort | solution.py:27
  139.8 3.8 %sort.92 = (s32[384]{0:T(512)}, s32[384]{0:T(512)S(1)}) sort(s32[384]{0:T(512)S(1)} %get-tuple-element.16, s32[384]{0:T(512)S(1)} %iota.24), dimensions={0}, to_apply=%region_5.7 | sort | flops 3456 | bytes 6144 | tf_op jit(solution)/shard_map/jit(argsort)/sort | solution.py:28
  143.6 0.0 copy-start.1
  143.6 45.2 %all-to-all-done.1 = f32[2,384,768]{2,0,1:T(2,128)} async-done(((f32[2,384,768]{2,0,1:T(2,128)}), f32[2,384,768]{2,0,1:T(2,128)}, u32[]{:S(2)}, u32[]{:S(2)}) %all-to-all-start.1) | async-done | bytes 2359328 | tf_op jit(solution)/shard_map/all_to_all | solution.py:51
  188.8 6.3 %gather_fusion.3 = f32[384,2,768]{2,1,0:T(2,128)} fusion(f32[2,384,768]{2,0,1:T(2,128)} %all-to-all-done.1, s32[1024]{0:T(1024)S(1)} %pad_clamp_fusion), kind=kCustom, calls=%fused_computation.3.clone | custom fusion | bytes 4720128 | tf_op jit(solution)/shard_map/jit(_take)/gather | solution.py:29
  195.1 0.0 all-gather.6.cloned.1.call-done
  195.1 0.0 copy-done.1
  195.1 11.0 %fusion.4 = f32[2,1,1,384,768]{4,3,2,1,0:T(8,128)} fusion(f32[2,1,1,384,768]{4,3,2,1,0:T(8,128)} %param.9, f32[2,1,1,384,768]{4,3,2,1,0:T(8,128)S(1)} %copy-done.1, f32[384,2,768]{2,1,0:T(2,128)} %gather_fusion.3, f32[2,1,1,768,768]{4,3,0,2,1:T(8,128)} %all-gather.6.cloned.1.call-done, f32[2,768]{1,0:T(2,128)S(1)} %bitcast.47, ...), kind=kOutput, calls=%fused_computation.11 | convolution fusion | flops 5439356928 | bytes 14162304 | tf_op jit(solution)/shard_map/hrk,hkc->hrc/dot_general | solution.py:12
  (28 shorter events, 0.3 us)
Async XLA Ops:
  11.2 2.4 %copy-start = (f32[2,1,1,384,768]{4,3,2,1,0:T(8,128)S(1)}, f32[2,1,1,384,768]{4,3,2,1,0:T(8,128)}, u32[]{:S(2)}) copy-start(f32[2,1,1,384,768]{4,3,2,1,0:T(8,128)} %param.8) | copy-start | bytes 7077892
  25.1 60.8 %all-to-all-start = ((f32[2,384,768]{2,0,1:T(2,128)}), f32[2,384,768]{2,0,1:T(2,128)S(1)}, u32[]{:S(2)}, u32[]{:S(2)}) async-start(f32[2,384,768]{2,0,1:T(2,128)} %select_bitcast_fusion.1), calls=%async_computation | async-start | bytes 4718592 | tf_op jit(solution)/shard_map/all_to_all | solution.py:51
  33.5 75.5 %all-gather.4.cloned.1.call-start = ((), (), s32[]{:S(2)}) async-start(), calls=%async_computation.2 | async-start | bytes 7077888 | tf_op jit(solution)/shard_map/all_gather | solution.py:11
  94.4 0.8 copy-start.3
  94.4 4.7 %copy-start.4 = (f32[2,1,1,768]{3,2,1,0:T(1,128)S(1)}, f32[2,1,1,768]{3,2,1,0:T(1,128)}, u32[]{:S(2)}) copy-start(f32[2,1,1,768]{3,2,1,0:T(1,128)} %param.11) | copy-start | bytes 18436
  94.4 14.6 %copy-start.2 = (f32[2,384,768]{2,1,0:T(8,128)S(1)}, f32[2,384,768]{2,1,0:T(8,128)}, u32[]{:S(2)}) copy-start(f32[2,384,768]{2,1,0:T(8,128)} %fusion.5) | copy-start | bytes 7077892
  94.5 100.6 %all-gather.6.cloned.1.call-start = ((), (), s32[]{:S(2)}) async-start(), calls=%async_computation.3 | async-start | bytes 7077888 | tf_op jit(solution)/shard_map/all_gather | solution.py:11
  128.9 7.0 %copy-start.5 = (f32[2,1,1,768]{3,2,1,0:T(1,128)S(1)}, f32[2,1,1,768]{3,2,1,0:T(1,128)}, u32[]{:S(2)}) copy-start(f32[2,1,1,768]{3,2,1,0:T(1,128)} %param.10) | copy-start | bytes 18436
  128.9 59.9 %all-to-all-start.1 = ((f32[2,384,768]{2,0,1:T(2,128)}), f32[2,384,768]{2,0,1:T(2,128)}, u32[]{:S(2)}, u32[]{:S(2)}) async-start(f32[2,384,768]{2,0,1:T(2,128)} %select_bitcast_fusion), calls=%async_computation.1 | async-start | bytes 4718592 | tf_op jit(solution)/shard_map/all_to_all | solution.py:51
  143.6 51.5 %copy-start.1 = (f32[2,1,1,384,768]{4,3,2,1,0:T(8,128)S(1)}, f32[2,1,1,384,768]{4,3,2,1,0:T(8,128)}, u32[]{:S(2)}) copy-start(f32[2,1,1,384,768]{4,3,2,1,0:T(8,128)} %param.8) | copy-start | bytes 7077892
Sparse Core Ops, SparseCore 0:
  94.6 14.3 all-gather.3
  110.5 15.6 all-gather.5
where the time goes:
time: 213 us
  waiting for transfers between devices  100 us (47%)
  other arithmetic  32.7 us (15%)
  local copies, waits for them, and re-layouts  31.7 us (15%)
  matrix products  18.9 us (9%)
  starting transfers between devices  15.6 us (7%)
  between operations  13.6 us (6%)
    all_to_all x2, waiting for transfers between devices, crossing(): lax.all_to_all(pack_rows(turned, target_x * width_y + target_y), ('kx', '...  90 us
    dot_general x2, matrix products, ladder(): jnp.einsum('hrk,hkc->hrc', scaled, whole, precision=lax.Precision.HIGHEST...  18.9 us
    all_to_all x2, starting transfers between devices, crossing(): lax.all_to_all(pack_rows(turned, target_x * width_y + target_y), ('kx', '...  15.3 us
    gather x2, local copies, waits for them, and re-layouts, unpack_rows(): return jnp.take(data, inverse, axis=1)  11.5 us
    gather x2, local copies, waits for them, and re-layouts, pack_rows(): return jnp.take(data, row_order, axis=1)  10.4 us
    all_gather x2, waiting for transfers between devices, ladder(): whole = lax.all_gather(vertex_rows, 'af', axis=1, tiled=True)  9.83 us
    sort x2, other arithmetic, unpack_rows(): inverse = jnp.argsort(row_order, stable=True)  7.57 us
    sort x2, other arithmetic, unpack_rows(): row_order = jnp.argsort(anchor, stable=True)  7.57 us
  transfers between devices with their start and end apart: 4, of which 3 were waited for; matrix products, arithmetic and copies ran while one was open for 21% of the time, Pallas kernels for 0%

commit v1 on v0

--- a/solution.py
+++ b/solution.py
@@ -48,12 +48,20 @@
     target_y = (ky_index + shift_y) % width_y
     anchor_x = (kx_index - shift_x) % width_x
     anchor_y = (ky_index - shift_y) % width_y
-    arrived = lax.all_to_all(
-        pack_rows(turned, target_x * width_y + target_y),
-        ("kx", "ky"),
-        split_axis=1,
-        concat_axis=1,
-        tiled=True,
+    arrived = jnp.concatenate(
+        lax.all_to_all(
+            jnp.stack(
+                jnp.split(
+                    pack_rows(turned, target_x * width_y + target_y),
+                    lax.axis_size(("kx", "ky")),
+                    axis=1,
+                )
+            ),
+            ("kx", "ky"),
+            0,
+            0,
+        ),
+        axis=1,
     )
     return unpack_rows(arrived, anchor_x * width_y + anchor_y)
 

time: 213 us -> 234 us (1.099)
  local copies, waits for them, and re-layouts: 31.7 us -> 54.9 us
    unnamed x14 -> x46, local copies, waits for them, and re-layouts: 0.47 us -> 22.1 us
  transfers between devices with their start and end apart: 4 -> 4, of which waited for: 3 -> 3; matrix products, arithmetic and copies ran while one was open for 21% -> 24% of each run, Pallas kernels for 0% -> 0%
where the time goes in v1:
time: 234 us
  waiting for transfers between devices  100 us (43%)
  local copies, waits for them, and re-layouts  54.9 us (23%)
  other arithmetic  30.7 us (13%)
  matrix products  18.9 us (8%)
  starting transfers between devices  15.6 us (7%)
  between operations  13.6 us (6%)
    all_to_all x2, waiting for transfers between devices, crossing(): lax.all_to_all(jnp.stack(jnp.split(pack_rows(turned, target_x * width_y +...  90 us
    unnamed x46, local copies, waits for them, and re-layouts  22.1 us
    dot_general x2, matrix products, ladder(): jnp.einsum('hrk,hkc->hrc', scaled, whole, precision=lax.Precision.HIGHEST...  18.9 us
    all_to_all x2, starting transfers between devices, crossing(): lax.all_to_all(jnp.stack(jnp.split(pack_rows(turned, target_x * width_y +...  15.3 us
    gather x2, local copies, waits for them, and re-layouts, unpack_rows(): return jnp.take(data, inverse, axis=1)  11.6 us
    gather x2, local copies, waits for them, and re-layouts, pack_rows(): return jnp.take(data, row_order, axis=1)  10.4 us
    all_gather x2, waiting for transfers between devices, ladder(): whole = lax.all_gather(vertex_rows, 'af', axis=1, tiled=True)  9.83 us
    sort x2, other arithmetic, unpack_rows(): inverse = jnp.argsort(row_order, stable=True)  7.54 us
  transfers between devices with their start and end apart: 4, of which 3 were waited for; matrix products, arithmetic and copies ran while one was open for 24% of the time, Pallas kernels for 0%

profile of v1, /device:TPU:0, one launch (start us, length us, event | category | flops | bytes accessed | tf_op | source)
XLA Modules:
  0.0 234.0 jit_solution(387064974030265465)
XLA Ops:
  6.5 0.8 fusion.76
  7.4 3.8 %sort.87 = (s32[384]{0:T(512)}, s32[384]{0:T(512)S(1)}) sort(s32[384]{0:T(512)S(1)} %get-tuple-element.33, s32[384]{0:T(512)S(1)} %iota.19), dimensions={0}, to_apply=%region_0.1 | sort | flops 3456 | bytes 6144 | tf_op jit(solution)/shard_map/jit(argsort)/sort | solution.py:22
  11.2 1.9 slice_bitcast_fusion.1
  13.1 0.4 copy-done
  13.6 0.5 maximum_select_fusion
  14.1 3.2 %copy.10 = f32[2,384,768]{2,0,1:T(2,128)} copy(f32[2,384,768]{2,1,0:T(8,128)S(1)} %maximum_select_fusion) | data formatting | bytes 4718592 | tf_op jit(solution)/shard_map/jit(_where)/select_n | solution.py:46
  17.3 5.1 %gather_fusion = f32[384,2,768]{2,1,0:T(2,128)S(1)} fusion(f32[2,384,768]{2,0,1:T(2,128)} %copy.10, s32[1024]{0:T(1024)S(1)} %pad_clamp_fusion.3), kind=kCustom, calls=%fused_computation.clone | custom fusion | bytes 4720128 | tf_op jit(solution)/shard_map/jit(_take)/gather | solution.py:23
  22.4 1.8 select_bitcast_fusion.1
  24.1 0.7 fusion.43
  24.8 0.7 fusion.42
  25.5 0.7 fusion.41
  26.2 0.7 fusion.40
  26.8 0.7 fusion.39
  27.5 0.7 fusion.38
  28.2 0.7 fusion.37
  28.9 0.7 fusion.36
  29.5 0.7 fusion.35
  30.2 0.7 fusion.34
  30.9 0.7 fusion.33
  31.6 0.7 fusion.32
  32.2 0.7 fusion.31
  32.9 0.7 fusion.30
  33.6 0.7 fusion.29
  34.3 0.7 fusion.28
  35.0 8.3 %all-to-all-start = ((f32[16,2,24,768]{3,1,2,0:T(2,128)}), f32[16,2,24,768]{3,1,2,0:T(2,128)S(1)}, u32[]{:S(2)}, u32[]{:S(2)}) async-start(f32[16,2,24,768]{3,1,2,0:T(2,128)} %fusion.28), calls=%async_computation | async-start | bytes 4718592 | tf_op jit(solution)/shard_map/all_to_all | solution.py:52
  43.3 0.0 all-gather.4.cloned.1.call-start
  43.4 3.8 %sort.88 = (s32[384]{0:T(512)}, s32[384]{0:T(512)S(1)}) sort(s32[384]{0:T(512)S(1)} %get-tuple-element.32, s32[384]{0:T(512)S(1)} %iota.20), dimensions={0}, to_apply=%region_1.3 | sort | flops 3456 | bytes 6144 | tf_op jit(solution)/shard_map/jit(argsort)/sort | solution.py:27
  47.1 3.8 %sort.89 = (s32[384]{0:T(512)}, s32[384]{0:T(512)S(1)}) sort(s32[384]{0:T(512)S(1)} %get-tuple-element.13, s32[384]{0:T(512)S(1)} %iota.21), dimensions={0}, to_apply=%region_2.4 | sort | flops 3456 | bytes 6144 | tf_op jit(solution)/shard_map/jit(argsort)/sort | solution.py:28
  51.0 44.8 %all-to-all-done = f32[16,2,24,768]{3,1,2,0:T(2,128)S(1)} async-done(((f32[16,2,24,768]{3,1,2,0:T(2,128)}), f32[16,2,24,768]{3,1,2,0:T(2,128)S(1)}, u32[]{:S(2)}, u32[]{:S(2)}) %all-to-all-start) | async-done | bytes 2359328 | tf_op jit(solution)/shard_map/all_to_all | solution.py:52
  95.7 5.2 %gather_fusion.1 = f32[384,2,768]{2,1,0:T(2,128)} fusion(f32[2,384,768]{2,0,1:T(2,128)S(1)} %bitcast.181, s32[1024]{0:T(1024)S(1)} %pad_clamp_fusion.2), kind=kCustom, calls=%fused_computation.1.clone | custom fusion | bytes 4720128 | tf_op jit(solution)/shard_map/jit(_take)/gather | solution.py:29
  100.9 3.3 %fusion.5 = f32[2,384,768]{2,1,0:T(8,128)} fusion(f32[384,2,768]{2,1,0:T(2,128)} %gather_fusion.1, pred[384]{0:T(512)(128)(4,1)S(1)} %compare_and_fusion.2), kind=kLoop, calls=%fused_computation.16 | loop fusion | flops 589824 | bytes 4718976 | tf_op jit(solution)/shard_map/jit(_take)/select_n | solution.py:29
  104.3 0.2 all-gather.6.cloned.1.call-start
  104.5 0.5 all-gather.6.cloned.1.call-update
  105.2 3.8 %sort.90 = (s32[384]{0:T(512)}, s32[384]{0:T(512)S(1)}) sort(s32[384]{0:T(512)S(1)} %get-tuple-element.31, s32[384]{0:T(512)S(1)} %iota.22), dimensions={0}, to_apply=%region_3.5 | sort | flops 3456 | bytes 6144 | tf_op jit(solution)/shard_map/jit(argsort)/sort | solution.py:22
  109.0 9.8 %all-gather.4.cloned.1.call-done = f32[2,768,768]{2,1,0:T(8,128)} async-done(((f32[2,384,768]{2,1,0:T(8,128)}), f32[2,768,768]{2,1,0:T(8,128)}) %all-gather.4.cloned.1.call-update) | async-done | bytes 4718608 | tf_op jit(solution)/shard_map/all_gather | solution.py:11
  118.8 7.9 %fusion.6 = f32[2,384,768]{2,1,0:T(8,128)S(1)} fusion(f32[2,768,768]{2,1,0:T(8,128)} %all-gather.4.cloned.1.call-done, f32[2,384,768]{2,1,0:T(8,128)S(1)} %copy-done.2, f32[2,768]{1,0:T(2,128)S(1)} %bitcast.184), kind=kOutput, calls=%fused_computation.19 | convolution fusion | flops 5436407808 | bytes 9443328 | tf_op jit(solution)/shard_map/hrk,hkc->hrc/dot_general | solution.py:12
  126.7 0.2 fusion.74
  126.9 0.5 maximum_select_fusion.1
  127.4 3.2 %copy.14 = f32[2,384,768]{2,0,1:T(2,128)} copy(f32[2,384,768]{2,1,0:T(8,128)S(1)} %maximum_select_fusion.1) | data formatting | bytes 4718592 | tf_op jit(solution)/shard_map/jit(_where)/select_n | solution.py:46
  130.6 5.4 %gather_fusion.2 = f32[384,2,768]{2,1,0:T(2,128)S(1)} fusion(f32[2,384,768]{2,0,1:T(2,128)} %copy.14, s32[1024]{0:T(1024)S(1)} %pad_clamp_fusion.1), kind=kCustom, calls=%fused_computation.2.clone | custom fusion | bytes 4720128 | tf_op jit(solution)/shard_map/jit(_take)/gather | solution.py:23
  136.0 1.8 select_bitcast_fusion
  137.8 0.7 fusion.27
  138.4 0.7 fusion.26
  139.1 0.7 fusion.25
  139.8 0.7 fusion.24
  140.5 0.7 fusion.23
  141.1 0.7 fusion.22
  141.8 0.7 fusion.21
  142.5 0.7 fusion.20
  143.2 0.7 fusion.19
  143.8 0.7 fusion.18
  144.5 0.7 fusion.17
  145.2 0.7 fusion.16
  145.9 0.7 fusion.15
  146.6 0.7 fusion.14
  147.2 0.7 fusion.13
  147.9 0.7 fusion.12
  148.6 7.0 %all-to-all-start.1 = ((f32[16,2,24,768]{3,1,2,0:T(2,128)}), f32[16,2,24,768]{3,1,2,0:T(2,128)S(1)}, u32[]{:S(2)}, u32[]{:S(2)}) async-start(f32[16,2,24,768]{3,1,2,0:T(2,128)} %fusion.12), calls=%async_computation.1 | async-start | bytes 4718592 | tf_op jit(solution)/shard_map/all_to_all | solution.py:52
  155.6 3.8 %sort.91 = (s32[384]{0:T(512)}, s32[384]{0:T(512)S(1)}) sort(s32[384]{0:T(512)S(1)} %get-tuple-element.30, s32[384]{0:T(512)S(1)} %iota.23), dimensions={0}, to_apply=%region_4.6 | sort | flops 3456 | bytes 6144 | tf_op jit(solution)/shard_map/jit(argsort)/sort | solution.py:27
  159.3 3.8 %sort.92 = (s32[384]{0:T(512)}, s32[384]{0:T(512)S(1)}) sort(s32[384]{0:T(512)S(1)} %get-tuple-element.16, s32[384]{0:T(512)S(1)} %iota.24), dimensions={0}, to_apply=%region_5.7 | sort | flops 3456 | bytes 6144 | tf_op jit(solution)/shard_map/jit(argsort)/sort | solution.py:28
  163.1 45.3 %all-to-all-done.1 = f32[16,2,24,768]{3,1,2,0:T(2,128)S(1)} async-done(((f32[16,2,24,768]{3,1,2,0:T(2,128)}), f32[16,2,24,768]{3,1,2,0:T(2,128)S(1)}, u32[]{:S(2)}, u32[]{:S(2)}) %all-to-all-start.1) | async-done | bytes 2359328 | tf_op jit(solution)/shard_map/all_to_all | solution.py:52
  208.4 1.4 copy-done.3
  209.8 6.4 %gather_fusion.3 = f32[384,2,768]{2,1,0:T(2,128)} fusion(f32[2,384,768]{2,0,1:T(2,128)} %bitcast.182, s32[1024]{0:T(1024)S(1)} %pad_clamp_fusion), kind=kCustom, calls=%fused_computation.3.clone | custom fusion | bytes 4720128 | tf_op jit(solution)/shard_map/jit(_take)/gather | solution.py:29
  216.2 11.0 %fusion.4 = f32[2,1,1,384,768]{4,3,2,1,0:T(8,128)} fusion(f32[2,1,1,384,768]{4,3,2,1,0:T(8,128)} %param.9, f32[2,1,1,384,768]{4,3,2,1,0:T(8,128)S(1)} %copy-done.1, f32[384,2,768]{2,1,0:T(2,128)} %gather_fusion.3, f32[2,1,1,768,768]{4,3,0,2,1:T(8,128)} %all-gather.6.cloned.1.call-done, f32[2,768]{1,0:T(2,128)S(1)} %bitcast.183, ...), kind=kOutput, calls=%fused_computation.11 | convolution fusion | flops 5439356928 | bytes 14162304 | tf_op jit(solution)/shard_map/hrk,hkc->hrc/dot_general | solution.py:12
  (42 shorter events, 0.3 us)
Async XLA Ops:
  11.2 2.4 %copy-start = (f32[2,1,1,384,768]{4,3,2,1,0:T(8,128)S(1)}, f32[2,1,1,384,768]{4,3,2,1,0:T(8,128)}, u32[]{:S(2)}) copy-start(f32[2,1,1,384,768]{4,3,2,1,0:T(8,128)} %param.8) | copy-start | bytes 7077892
  35.0 60.8 %all-to-all-start = ((f32[16,2,24,768]{3,1,2,0:T(2,128)}), f32[16,2,24,768]{3,1,2,0:T(2,128)S(1)}, u32[]{:S(2)}, u32[]{:S(2)}) async-start(f32[16,2,24,768]{3,1,2,0:T(2,128)} %fusion.28), calls=%async_computation | async-start | bytes 4718592 | tf_op jit(solution)/shard_map/all_to_all | solution.py:52
  43.3 75.5 %all-gather.4.cloned.1.call-start = ((), (), s32[]{:S(2)}) async-start(), calls=%async_computation.2 | async-start | bytes 7077888 | tf_op jit(solution)/shard_map/all_gather | solution.py:11
  104.3 0.8 copy-start.4
  104.3 4.7 %copy-start.5 = (f32[2,1,1,768]{3,2,1,0:T(1,128)S(1)}, f32[2,1,1,768]{3,2,1,0:T(1,128)}, u32[]{:S(2)}) copy-start(f32[2,1,1,768]{3,2,1,0:T(1,128)} %param.11) | copy-start | bytes 18436
  104.3 14.6 %copy-start.2 = (f32[2,384,768]{2,1,0:T(8,128)S(1)}, f32[2,384,768]{2,1,0:T(8,128)}, u32[]{:S(2)}) copy-start(f32[2,384,768]{2,1,0:T(8,128)} %fusion.5) | copy-start | bytes 7077892
  104.3 111.9 %all-gather.6.cloned.1.call-start = ((), (), s32[]{:S(2)}) async-start(), calls=%async_computation.3 | async-start | bytes 7077888 | tf_op jit(solution)/shard_map/all_gather | solution.py:11
  148.6 7.0 %copy-start.6 = (f32[2,1,1,768]{3,2,1,0:T(1,128)S(1)}, f32[2,1,1,768]{3,2,1,0:T(1,128)}, u32[]{:S(2)}) copy-start(f32[2,1,1,768]{3,2,1,0:T(1,128)} %param.10) | copy-start | bytes 18436
  148.6 59.8 %all-to-all-start.1 = ((f32[16,2,24,768]{3,1,2,0:T(2,128)}), f32[16,2,24,768]{3,1,2,0:T(2,128)S(1)}, u32[]{:S(2)}, u32[]{:S(2)}) async-start(f32[16,2,24,768]{3,1,2,0:T(2,128)} %fusion.12), calls=%async_computation.1 | async-start | bytes 4718592 | tf_op jit(solution)/shard_map/all_to_all | solution.py:52
  208.4 1.4 copy-start.3
  209.8 6.4 %copy-start.1 = (f32[2,1,1,384,768]{4,3,2,1,0:T(8,128)S(1)}, f32[2,1,1,384,768]{4,3,2,1,0:T(8,128)}, u32[]{:S(2)}) copy-start(f32[2,1,1,384,768]{4,3,2,1,0:T(8,128)} %param.8) | copy-start | bytes 7077892
Sparse Core Ops, SparseCore 0:
  104.4 14.3 all-gather.3
  120.4 15.6 all-gather.5
